TPU v7x, 32 devices: a whole 2x2x4 slice. The times are simulated.
32 devices in a mesh: dom: 4 (over z), blk: 8 (over y, x, core).
Axes of the slice: x: 2, y: 2, z: 4, core: 2. Of those that a mesh axis runs over, the one named last changes fastest.
Arguments:
- features: bfloat16 [16384, 128], P(('dom', 'blk')), may hold values from -6 to 6
- history: bfloat16 [16384, 512], P(('dom', 'blk')), may hold values from 0 to 1.5
- adj_tiles: bfloat16 [16384, 4, 512], P(('dom', 'blk')), may hold values from -0.109375 to 0.109375
- tile_cols: int32 [4, 8, 4], P('dom', 'blk'), may hold values from 0 to 7, as said below
- bound_one: bfloat16 [16384, 1024], P(('dom', 'blk')), may hold values from -0.109375 to 0.109375
- bound_two: bfloat16 [16384, 1024], P(('dom', 'blk')), may hold values from -0.109375 to 0.109375
- block_ids: int32 [2, 4, 8, 4, 2], P(None, 'dom', 'blk'), may hold values from 0 to 3
- block_counts: int32 [2, 4, 8, 4], P(None, 'dom', 'blk'), may hold values from 0 to 2, as said below
- w_in: bfloat16 [128, 512], replicated, may hold values from -0.5 to 0.5
- b_in: float32 [512], replicated, may hold values from -3 to 3
- w_out: bfloat16 [512, 512], replicated, may hold values from -0.25 to 0.25
- b_out: float32 [512], replicated, may hold values from -3 to 3
Outputs:
- fresh_history: bfloat16 [16384, 512], P(('dom', 'blk'))
- node_out: bfloat16 [16384, 512], P(('dom', 'blk'))
Inputs may be any that keep to these rules, and one draw needn't show every extreme that they name: `tile_cols`: each device's list names 4 distinct blk indices, its own first. `block_counts`: zero where owner and reader are the same partition; for every layer and reader partition some blk index receives 2 live slots from every other partition.
All inputs are finite; a program needn't handle non-finite values.
Results may differ from a plain program's by a relative error of at most 0.0055.
Values may be sent and summed in bfloat16 or wider, within the bound.
No kernel may reach another device: no remote copies, remote signals or barrier semaphores. Data moves between devices by JAX's collectives and lax.ppermute only.
A program may use at most 64 MiB of HBM per device.

v0:
```python
import functools

import jax
import jax.numpy as jnp
from jax import lax
from jax.experimental import pallas as pl
from jax.experimental.pallas import tpu as pltpu
from jax.sharding import PartitionSpec as P


BF16 = jnp.bfloat16
F32 = jnp.float32
VMEM = pl.BlockSpec(memory_space=pltpu.VMEM)
MIB = 1 << 20
SMEM = pl.BlockSpec(memory_space=pltpu.SMEM)


def near(array):
    return pltpu.with_memory_space_constraint(array, pltpu.VMEM)


def dot(a, b):
    return jnp.dot(a, b, preferred_element_type=F32)


def pack_kernel(layer, ids_ref, counts_ref, panel_ref, *out_refs):
    slots, n_dom = ids_ref.shape[-2:]
    rows = out_refs[0].shape[0] // slots
    dom = lax.axis_index("dom")
    for shift, out_ref in enumerate(out_refs, 1):
        reader = lax.rem(dom + shift, n_dom)
        live = counts_ref[layer, 0, 0, reader]
        for slot in range(slots):
            start = pl.multiple_of(ids_ref[layer, 0, 0, slot, reader] * rows, rows)
            here = pl.ds(slot * rows, rows)

            @pl.when(slot < live)
            def _():
                out_ref[here, :] = panel_ref[pl.ds(start, rows), :]

            @pl.when(slot >= live)
            def _():
                out_ref[here, :] = jnp.zeros((rows, out_ref.shape[1]), out_ref.dtype)


def pack(layer, ids, counts, panel, slot_rows):
    n_dom = ids.shape[-1]
    return pl.pallas_call(
        functools.partial(pack_kernel, layer),
        out_shape=[pltpu.VMEM((slot_rows, panel.shape[1]), panel.dtype)] * (n_dom - 1),
        in_specs=[SMEM, SMEM, VMEM],
        out_specs=[VMEM] * (n_dom - 1),
        compiler_params=pltpu.CompilerParams(vmem_limit_bytes=MIB),
    )(ids, counts, near(panel))


def pick_panels(blk, cols_ref, panel_refs, chosen_ref):
    occupied = cols_ref.shape[-1]
    chosen_ref[0] = panel_refs[0][...]
    for k in range(1, occupied):
        apart = lax.bitwise_xor(cols_ref[0, 0, k], blk)
        for d, panel_ref in enumerate(panel_refs):
            @pl.when(apart == d)
            def _():
                chosen_ref[k] = panel_ref[...]


def border_product(dom, bound_ref, border_refs, shifts):
    n_dom = bound_ref.shape[1] // border_refs[0].shape[0]
    total = None
    for border_ref, shift in zip(border_refs, shifts):
        width = border_ref.shape[0]
        owner = lax.rem(dom + n_dom - shift, n_dom)
        part = dot(bound_ref[:, pl.ds(pl.multiple_of(owner * width, width), width)], border_ref[...])
        total = part if total is None else total + part
    return total


def first_kernel(n_blk, cols_ref, tiles_ref, bound_ref, *refs):
    panel_refs, border_refs = refs[:n_blk], refs[n_blk:-2]
    agg_ref, chosen_ref = refs[-2:]
    pick_panels(lax.axis_index("blk"), cols_ref, panel_refs, chosen_ref)
    total = border_product(lax.axis_index("dom"), bound_ref, border_refs, range(1, len(border_refs) + 1))
    for k in range(cols_ref.shape[-1]):
        total = total + dot(tiles_ref[k], chosen_ref[k])
    agg_ref[...] = total.astype(BF16)


def first_layer(cols, tiles, bound, panels, border):
    shape = panels[0].shape
    return pl.pallas_call(
        functools.partial(first_kernel, len(panels)),
        out_shape=pltpu.VMEM(shape, BF16),
        in_specs=[SMEM] + [VMEM] * (2 + len(panels) + len(border)),
        out_specs=VMEM,
        scratch_shapes=[pltpu.VMEM((cols.shape[-1],) + shape, BF16)],
        compiler_params=pltpu.CompilerParams(vmem_limit_bytes=8 * MIB),
        name="first",
    )(cols, *map(near, (tiles, bound, *panels, *border)))


def inside_kernel(n_blk, cols_ref, tiles_ref, w_ref, b_ref, *refs):
    panel_refs = refs[:n_blk]
    fresh_ref, total_ref, chosen_ref = refs[n_blk:]
    pick_panels(lax.axis_index("blk"), cols_ref, panel_refs, chosen_ref)
    total = None
    for k in range(cols_ref.shape[-1]):
        fresh = jnp.maximum(dot(chosen_ref[k], w_ref[...]) + b_ref[...], 0.0).astype(BF16)
        if k == 0:
            fresh_ref[...] = fresh
        part = dot(tiles_ref[k], fresh)
        total = part if total is None else total + part
    total_ref[...] = total


def inside(cols, tiles, w_in, b_in, panels):
    shape = panels[0].shape
    rows, width = shape[0], w_in.shape[1]
    return pl.pallas_call(
        functools.partial(inside_kernel, len(panels)),
        out_shape=[jax.ShapeDtypeStruct((rows, width), BF16), pltpu.VMEM((rows, width), F32)],
        in_specs=[SMEM] + [VMEM] * (3 + len(panels)),
        out_specs=[VMEM, VMEM],
        scratch_shapes=[pltpu.VMEM((cols.shape[-1],) + shape, BF16)],
        compiler_params=pltpu.CompilerParams(vmem_limit_bytes=12 * MIB),
        name="inside",
    )(cols, *map(near, (tiles, w_in, b_in, *panels)))


def last_kernel(total_ref, bound_ref, w_ref, b_ref, *refs):
    border_refs, out_ref = refs[:-1], refs[-1]
    total = total_ref[...] + border_product(lax.axis_index("dom"), bound_ref, border_refs, range(1, len(border_refs) + 1))
    out_ref[...] = (dot(total.astype(BF16), w_ref[...]) + b_ref[...]).astype(BF16)


def last_layer(total, bound, w_out, b_out, border):
    return pl.pallas_call(
        last_kernel,
        out_shape=jax.ShapeDtypeStruct((total.shape[0], w_out.shape[1]), BF16),
        in_specs=[VMEM] * (4 + len(border)),
        out_specs=VMEM,
        compiler_params=pltpu.CompilerParams(vmem_limit_bytes=8 * MIB),
        name="last",
    )(*map(near, (total, bound, w_out, b_out, *border)))


def swap(block, apart):
    n_blk = lax.axis_size("blk")
    return lax.ppermute(block, "blk", [(i, i ^ apart) for i in range(n_blk)])


def send_on(block, shift):
    n_dom = lax.axis_size("dom")
    return lax.ppermute(block, "dom", [(i, (i + shift) % n_dom) for i in range(n_dom)])


def all_panels(panel):
    n_blk = lax.axis_size("blk")
    panels = {0: panel}
    far = sorted(range(2, n_blk, 2), key=lambda d: -bin(d).count("1"))
    for d in far:
        panels[d] = swap(panel, d)
    panels[1] = swap(panel, 1)
    for d in far:
        panels[d + 1] = swap(panels[d], 1)
    return [panels[d] for d in range(n_blk)]


def borders(layer, ids, counts, panel, slot_rows):
    blocks = pack(layer, ids, counts, panel, slot_rows)
    return [send_on(block, s) for s, block in enumerate(blocks, 1)]


def body(features, history, adj_tiles, tile_cols, bound_one, bound_two, block_ids, block_counts, w_in, b_in, w_out, b_out):
    slot_rows = bound_one.shape[1] // lax.axis_size("dom")
    ids = block_ids.swapaxes(3, 4)
    panels_one = all_panels(features)
    border_one = borders(0, ids, block_counts, features, slot_rows)
    border_two = borders(1, ids, block_counts, history, slot_rows)
    tiles = adj_tiles.transpose(1, 0, 2)
    agg = first_layer(tile_cols, tiles, bound_one, panels_one, border_one)
    panels_two = all_panels(agg)
    fresh, total = inside(tile_cols, tiles, w_in, b_in.reshape(1, -1), panels_two)
    out = last_layer(total, bound_two, w_out, b_out.reshape(1, -1), border_two)
    return fresh, out


def solution(mesh):
    rows = P(("dom", "blk"), None)
    placed = (
        rows,
        rows,
        P(("dom", "blk"), None, None),
        P("dom", "blk", None),
        rows,
        rows,
        P(None, "dom", "blk", None, None),
        P(None, "dom", "blk", None),
        P(),
        P(),
        P(),
        P(),
    )
    return jax.shard_map(body, mesh=mesh, in_specs=placed, out_specs=(rows, rows), check_vma=False)
```

profile of v0, /device:TPU:15, one launch (start us, length us, event | category | flops | bytes accessed | tf_op | source)
XLA Modules:
  0.0 58.4 jit_solution(2901112979232843346)
XLA Ops:
  0.6 0.3 collective-permute-start.1
  0.9 0.2 collective-permute-start.3
  1.2 2.2 %collective-permute-start.5 = (bf16[512,128]{1,0:T(8,128)(2,1)}, bf16[512,128]{1,0:T(8,128)(2,1)S(1)}, u32[]{:S(2)}, u32[]{:S(2)}) collective-permute-start(bf16[512,128]{1,0:T(8,128)(2,1)} %refs_0_.1), channel_id=1, source_target_pairs={{0,6},{1,7},{2,4},{3,5},{4,2},{5,3},{6,0},{7,1},{8,14},{9,15},{10,... | collective-permute-start | bytes 393224 | tf_op jit(solution)/shard_map/ppermute | solution.py:149
  3.3 0.9 %copy-done.3 = bf16[512,128]{1,0:T(8,128)(2,1)S(1)} copy-done((bf16[512,128]{1,0:T(8,128)(2,1)S(1)}, bf16[512,128]{1,0:T(8,128)(2,1)}, u32[]{:S(2)}) %copy-start.3) | copy-done | bytes 131096
  4.3 0.7 %copy-done.7 = s32[2,1,1,4,2]{3,4,2,1,0:T(2,128)S(1)} copy-done((s32[2,1,1,4,2]{3,4,2,1,0:T(2,128)S(1)}, s32[2,1,1,4,2]{3,4,2,1,0:T(2,128)}, u32[]{:S(2)}) %copy-start.7) | copy-done | bytes 88
  5.0 0.7 %copy-done.9 = s32[2,1,1,4]{3,2,1,0:T(1,128)S(1)} copy-done((s32[2,1,1,4]{3,2,1,0:T(1,128)S(1)}, s32[2,1,1,4]{3,2,1,0:T(1,128)}, u32[]{:S(2)}) %copy-start.9) | copy-done | bytes 56
  5.6 0.7 %shard_map.131 = (bf16[256,128]{1,0:T(8,128)(2,1)S(1)}, bf16[256,128]{1,0:T(8,128)(2,1)S(1)}, bf16[256,128]{1,0:T(8,128)(2,1)S(1)}) custom-call(s32[2,1,1,2,4]{4,3,2,1,0:T(2,128)S(1)} %bitcast.8, s32[2,1,1,4]{3,2,1,0:T(1,128)S(1)} %copy-done.9, bf16[512,128]{1,0:T(8,128)(2,1)S(1)} %copy-done.3), custom_call_target="tpu_custom_call" | custom-call | tf_op jit(solution)/shard_map/pallas_call | solution.py:48
  6.3 1.4 %collective-permute-start.7 = (bf16[256,128]{1,0:T(8,128)(2,1)S(1)}, bf16[256,128]{1,0:T(8,128)(2,1)S(1)}, u32[]{:S(2)}, u32[]{:S(2)}) collective-permute-start(bf16[256,128]{1,0:T(8,128)(2,1)S(1)} %get-tuple-element.10), channel_id=1, source_target_pairs={{0,8},{8,16},{16,24},{24,0},{1,9},{9,17},{17,25},{25,1},{2,10},{10... | collective-permute-start | bytes 196616 | tf_op jit(solution)/shard_map/ppermute | solution.py:154
  7.7 1.8 %collective-permute-start = (bf16[512,128]{1,0:T(8,128)(2,1)}, bf16[512,128]{1,0:T(8,128)(2,1)S(1)}, u32[]{:S(2)}, u32[]{:S(2)}) collective-permute-start(bf16[512,128]{1,0:T(8,128)(2,1)} %refs_0_.1), channel_id=1, source_target_pairs={{0,1},{1,0},{2,3},{3,2},{4,5},{5,4},{6,7},{7,6},{8,9},{9,8},{10,11... | collective-permute-start | bytes 393224 | tf_op jit(solution)/shard_map/ppermute | solution.py:149
  9.5 0.0 collective-permute-done.7.refs_8_
  9.5 2.3 %collective-permute-start.8 = (bf16[256,128]{1,0:T(8,128)(2,1)S(1)}, bf16[256,128]{1,0:T(8,128)(2,1)S(1)}, u32[]{:S(2)}, u32[]{:S(2)}) collective-permute-start(bf16[256,128]{1,0:T(8,128)(2,1)S(1)} %get-tuple-element.11), channel_id=1, source_target_pairs={{0,16},{8,24},{16,0},{24,8},{1,17},{9,25},{17,1},{25,9},{2,18},{10... | collective-permute-start | bytes 196616 | tf_op jit(solution)/shard_map/ppermute | solution.py:154
  11.8 0.0 collective-permute-done.1.refs_2_
  11.8 2.9 %collective-permute-start.2 = (bf16[512,128]{1,0:T(8,128)(2,1)S(1)}, bf16[512,128]{1,0:T(8,128)(2,1)S(1)}, u32[]{:S(2)}, u32[]{:S(2)}) collective-permute-start(bf16[512,128]{1,0:T(8,128)(2,1)S(1)} %collective-permute-done.1.refs_2_), channel_id=1, source_target_pairs={{0,1},{1,0},{2,3},{3,2},{4,5},{5,4},{6,7},{7,6},{8,9},{9,8},{10,11... | collective-permute-start | bytes 393224 | tf_op jit(solution)/shard_map/ppermute | solution.py:149
  14.7 0.0 collective-permute-done.3.refs_4_
  14.8 0.1 collective-permute-start.4
  14.8 0.0 collective-permute-done.5.refs_6_
  14.8 0.4 collective-permute-start.6
  15.3 0.0 collective-permute-done.8.refs_9_
  15.3 0.3 collective-permute-start.9
  15.5 2.1 %copy.16 = bf16[512,4,512]{2,0,1:T(8,128)(2,1)S(1)} copy(bf16[512,4,512]{2,1,0:T(4,128)(2,1)} %param.14) | data formatting | bytes 4194304 | tf_op args[2]
  17.6 0.8 %collective-permute-done.9.refs_10_ = bf16[256,128]{1,0:T(8,128)(2,1)S(1)} collective-permute-done((bf16[256,128]{1,0:T(8,128)(2,1)S(1)}, bf16[256,128]{1,0:T(8,128)(2,1)S(1)}, u32[]{:S(2)}, u32[]{:S(2)}) %collective-permute-start.9) | collective-permute-done | bytes 65568 | tf_op jit(solution)/shard_map/ppermute | solution.py:154
  18.5 0.0 collective-permute-done.refs_1_
  18.5 0.0 collective-permute-done.2.refs_3_
  18.5 0.0 collective-permute-done.4.refs_5_
  18.5 0.0 collective-permute-done.6.refs_7_
  18.5 0.0 copy-done
  18.5 0.0 copy-done.4
  18.5 0.0 copy-done.13
  18.5 0.0 copy-start.5
  18.5 0.0 copy-start.8
  18.5 0.0 copy-start.10
  18.5 0.0 copy-start.6
  18.6 0.0 copy-start.12
  18.6 1.6 %first.1.refs_0_ = bf16[512,128]{1,0:T(8,128)(2,1)S(1)} custom-call(s32[1,1,4]{2,1,0:T(1,128)S(1)} %copy-done.13, bf16[4,512,512]{2,1,0:T(8,128)(2,1)S(1)} %bitcast.6, bf16[512,1024]{1,0:T(8,128)(2,1)S(1)} %copy-done, bf16[512,128]{1,0:T(8,128)(2,1)S(1)} %copy-done.4, bf16[512,128]{1,0:T(8,128)(2,1)S(1)} %collective-permute-done.refs_1_, ...), custom_call_target="tpu_custom_call" | custom-call | tf_op jit(solution)/shard_map/first/pallas_call | solution.py:91
  20.2 0.0 copy-start.1
  20.2 0.0 copy-start.2
  20.2 0.0 copy-start.11
  20.2 0.3 collective-permute-start.11
  20.5 0.2 collective-permute-start.13
  20.8 2.2 %collective-permute-start.15 = (bf16[512,128]{1,0:T(8,128)(2,1)S(1)}, bf16[512,128]{1,0:T(8,128)(2,1)S(1)}, u32[]{:S(2)}, u32[]{:S(2)}) collective-permute-start(bf16[512,128]{1,0:T(8,128)(2,1)S(1)} %first.1.refs_0_), channel_id=1, source_target_pairs={{0,6},{1,7},{2,4},{3,5},{4,2},{5,3},{6,0},{7,1},{8,14},{9,15},{10,... | collective-permute-start | bytes 393224 | tf_op jit(solution)/shard_map/ppermute | solution.py:149
  22.9 0.0 copy-done.5
  22.9 0.0 copy-done.8
  22.9 0.0 copy-done.10
  22.9 0.7 %shard_map.132 = (bf16[256,512]{1,0:T(8,128)(2,1)S(1)}, bf16[256,512]{1,0:T(8,128)(2,1)S(1)}, bf16[256,512]{1,0:T(8,128)(2,1)S(1)}) custom-call(s32[2,1,1,2,4]{4,3,2,1,0:T(2,128)S(1)} %bitcast.9, s32[2,1,1,4]{3,2,1,0:T(1,128)S(1)} %copy-done.10, bf16[512,512]{1,0:T(8,128)(2,1)S(1)} %copy-done.5), custom_call_target="tpu_custom_call" | custom-call | tf_op jit(solution)/shard_map/pallas_call | solution.py:48
  23.6 4.1 %collective-permute-start.10 = (bf16[512,128]{1,0:T(8,128)(2,1)S(1)}, bf16[512,128]{1,0:T(8,128)(2,1)S(1)}, u32[]{:S(2)}, u32[]{:S(2)}) collective-permute-start(bf16[512,128]{1,0:T(8,128)(2,1)S(1)} %first.1.refs_0_), channel_id=1, source_target_pairs={{0,1},{1,0},{2,3},{3,2},{4,5},{5,4},{6,7},{7,6},{8,9},{9,8},{10,11... | collective-permute-start | bytes 393224 | tf_op jit(solution)/shard_map/ppermute | solution.py:149
  27.8 0.0 collective-permute-done.11.refs_2_
  27.8 0.7 %collective-permute-start.12 = (bf16[512,128]{1,0:T(8,128)(2,1)S(1)}, bf16[512,128]{1,0:T(8,128)(2,1)S(1)}, u32[]{:S(2)}, u32[]{:S(2)}) collective-permute-start(bf16[512,128]{1,0:T(8,128)(2,1)S(1)} %collective-permute-done.11.refs_2_), channel_id=1, source_target_pairs={{0,1},{1,0},{2,3},{3,2},{4,5},{5,4},{6,7},{7,6},{8,9},{9,8},{10,11... | collective-permute-start | bytes 393224 | tf_op jit(solution)/shard_map/ppermute | solution.py:149
  28.5 1.4 %collective-permute-start.17 = (bf16[256,512]{1,0:T(8,128)(2,1)S(1)}, bf16[256,512]{1,0:T(8,128)(2,1)S(1)}, u32[]{:S(2)}, u32[]{:S(2)}) collective-permute-start(bf16[256,512]{1,0:T(8,128)(2,1)S(1)} %get-tuple-element.15), channel_id=1, source_target_pairs={{0,8},{8,16},{16,24},{24,0},{1,9},{9,17},{17,25},{25,1},{2,10},{10... | collective-permute-start | bytes 786440 | tf_op jit(solution)/shard_map/ppermute | solution.py:154
  29.8 0.0 collective-permute-done.13.refs_4_
  29.8 3.3 %collective-permute-start.18 = (bf16[256,512]{1,0:T(8,128)(2,1)S(1)}, bf16[256,512]{1,0:T(8,128)(2,1)S(1)}, u32[]{:S(2)}, u32[]{:S(2)}) collective-permute-start(bf16[256,512]{1,0:T(8,128)(2,1)S(1)} %get-tuple-element.16), channel_id=1, source_target_pairs={{0,16},{8,24},{16,0},{24,8},{1,17},{9,25},{17,1},{25,9},{2,18},{10... | collective-permute-start | bytes 786440 | tf_op jit(solution)/shard_map/ppermute | solution.py:154
  33.1 0.0 collective-permute-done.15.refs_6_
  33.1 1.5 %collective-permute-start.19 = (bf16[256,512]{1,0:T(8,128)(2,1)S(1)}, bf16[256,512]{1,0:T(8,128)(2,1)S(1)}, u32[]{:S(2)}, u32[]{:S(2)}) collective-permute-start(bf16[256,512]{1,0:T(8,128)(2,1)S(1)} %get-tuple-element.17), channel_id=1, source_target_pairs={{0,24},{8,0},{16,8},{24,16},{1,25},{9,1},{17,9},{25,17},{2,26},{10... | collective-permute-start | bytes 786440 | tf_op jit(solution)/shard_map/ppermute | solution.py:154
  34.6 0.0 collective-permute-done.10.refs_1_
  34.6 0.8 %collective-permute-start.14 = (bf16[512,128]{1,0:T(8,128)(2,1)S(1)}, bf16[512,128]{1,0:T(8,128)(2,1)S(1)}, u32[]{:S(2)}, u32[]{:S(2)}) collective-permute-start(bf16[512,128]{1,0:T(8,128)(2,1)S(1)} %collective-permute-done.13.refs_4_), channel_id=1, source_target_pairs={{0,1},{1,0},{2,3},{3,2},{4,5},{5,4},{6,7},{7,6},{8,9},{9,8},{10,11... | collective-permute-start | bytes 393224 | tf_op jit(solution)/shard_map/ppermute | solution.py:149
  35.4 0.0 collective-permute-done.12.refs_3_
  35.4 0.1 collective-permute-start.16
  35.5 0.9 %collective-permute-done.14.refs_5_ = bf16[512,128]{1,0:T(8,128)(2,1)S(1)} collective-permute-done((bf16[512,128]{1,0:T(8,128)(2,1)S(1)}, bf16[512,128]{1,0:T(8,128)(2,1)S(1)}, u32[]{:S(2)}, u32[]{:S(2)}) %collective-permute-start.14) | collective-permute-done | bytes 131104 | tf_op jit(solution)/shard_map/ppermute | solution.py:149
  36.4 0.4 collective-permute-done.16.refs_7_
  36.8 0.0 copy-done.12
  36.8 2.7 %inside.1 = (bf16[512,512]{1,0:T(8,128)(2,1)}, f32[512,512]{1,0:T(8,128)S(1)}) custom-call(s32[1,1,4]{2,1,0:T(1,128)S(1)} %copy-done.13, bf16[4,512,512]{2,1,0:T(8,128)(2,1)S(1)} %bitcast.7, bf16[128,512]{1,0:T(8,128)(2,1)S(1)} %copy-done.6, f32[1,512]{1,0:T(1,128)S(1)} %bitcast.11, bf16[512,128]{1,0:T(8,128)(2,1)S(1)} %first.1.refs_0_, ...), custom_call_target="tpu_custom_call" | custom-call | tf_op jit(solution)/shard_map/inside/pallas_call | solution.py:119
  39.4 0.0 collective-permute-done.17.refs_0_
  39.5 12.9 %collective-permute-done.18.refs_1_ = bf16[256,512]{1,0:T(8,128)(2,1)S(1)} collective-permute-done((bf16[256,512]{1,0:T(8,128)(2,1)S(1)}, bf16[256,512]{1,0:T(8,128)(2,1)S(1)}, u32[]{:S(2)}, u32[]{:S(2)}) %collective-permute-start.18) | collective-permute-done | bytes 262176 | tf_op jit(solution)/shard_map/ppermute | solution.py:154
  52.3 4.5 %collective-permute-done.19.refs_2_ = bf16[256,512]{1,0:T(8,128)(2,1)S(1)} collective-permute-done((bf16[256,512]{1,0:T(8,128)(2,1)S(1)}, bf16[256,512]{1,0:T(8,128)(2,1)S(1)}, u32[]{:S(2)}, u32[]{:S(2)}) %collective-permute-start.19) | collective-permute-done | bytes 262176 | tf_op jit(solution)/shard_map/ppermute | solution.py:154
  56.8 1.6 %last.1 = bf16[512,512]{1,0:T(8,128)(2,1)} custom-call(f32[512,512]{1,0:T(8,128)S(1)} %get-tuple-element.14.total_ref, bf16[512,1024]{1,0:T(8,128)(2,1)S(1)} %copy-done.1, bf16[512,512]{1,0:T(8,128)(2,1)S(1)} %copy-done.2, f32[1,512]{1,0:T(1,128)S(1)} %bitcast.10, bf16[256,512]{1,0:T(8,128)(2,1)S(1)} %collective-permute-done.17.refs_0_, ...), custom_call_target="tpu_custom_call" | custom-call | tf_op jit(solution)/shard_map/last/pallas_call | solution.py:137
  (10 shorter events, 0.0 us)
Async XLA Ops:
  0.6 11.2 %collective-permute-start.1 = (bf16[512,128]{1,0:T(8,128)(2,1)}, bf16[512,128]{1,0:T(8,128)(2,1)S(1)}, u32[]{:S(2)}, u32[]{:S(2)}) collective-permute-start(bf16[512,128]{1,0:T(8,128)(2,1)} %refs_0_.1), channel_id=1, source_target_pairs={{0,2},{1,3},{2,0},{3,1},{4,6},{5,7},{6,4},{7,5},{8,10},{9,11},{10,... | collective-permute-start | bytes 393224 | tf_op jit(solution)/shard_map/ppermute | solution.py:149
  0.9 13.8 %collective-permute-start.3 = (bf16[512,128]{1,0:T(8,128)(2,1)}, bf16[512,128]{1,0:T(8,128)(2,1)S(1)}, u32[]{:S(2)}, u32[]{:S(2)}) collective-permute-start(bf16[512,128]{1,0:T(8,128)(2,1)} %refs_0_.1), channel_id=1, source_target_pairs={{0,4},{1,5},{2,6},{3,7},{4,0},{5,1},{6,2},{7,3},{8,12},{9,13},{10,... | collective-permute-start | bytes 393224 | tf_op jit(solution)/shard_map/ppermute | solution.py:149
  1.2 13.6 %collective-permute-start.5 = (bf16[512,128]{1,0:T(8,128)(2,1)}, bf16[512,128]{1,0:T(8,128)(2,1)S(1)}, u32[]{:S(2)}, u32[]{:S(2)}) collective-permute-start(bf16[512,128]{1,0:T(8,128)(2,1)} %refs_0_.1), channel_id=1, source_target_pairs={{0,6},{1,7},{2,4},{3,5},{4,2},{5,3},{6,0},{7,1},{8,14},{9,15},{10,... | collective-permute-start | bytes 393224 | tf_op jit(solution)/shard_map/ppermute | solution.py:149
  3.3 0.9 %copy-start.3 = (bf16[512,128]{1,0:T(8,128)(2,1)S(1)}, bf16[512,128]{1,0:T(8,128)(2,1)}, u32[]{:S(2)}) copy-start(bf16[512,128]{1,0:T(8,128)(2,1)} %refs_0_.1) | copy-start | bytes 393220
  4.3 0.7 %copy-start.7 = (s32[2,1,1,4,2]{3,4,2,1,0:T(2,128)S(1)}, s32[2,1,1,4,2]{3,4,2,1,0:T(2,128)}, u32[]{:S(2)}) copy-start(s32[2,1,1,4,2]{3,4,2,1,0:T(2,128)} %param.18) | copy-start | bytes 196
  5.0 0.7 %copy-start.9 = (s32[2,1,1,4]{3,2,1,0:T(1,128)S(1)}, s32[2,1,1,4]{3,2,1,0:T(1,128)}, u32[]{:S(2)}) copy-start(s32[2,1,1,4]{3,2,1,0:T(1,128)} %counts_ref.3) | copy-start | bytes 100
  6.3 3.2 %collective-permute-start.7 = (bf16[256,128]{1,0:T(8,128)(2,1)S(1)}, bf16[256,128]{1,0:T(8,128)(2,1)S(1)}, u32[]{:S(2)}, u32[]{:S(2)}) collective-permute-start(bf16[256,128]{1,0:T(8,128)(2,1)S(1)} %get-tuple-element.10), channel_id=1, source_target_pairs={{0,8},{8,16},{16,24},{24,0},{1,9},{9,17},{17,25},{25,1},{2,10},{10... | collective-permute-start | bytes 196616 | tf_op jit(solution)/shard_map/ppermute | solution.py:154
  7.7 10.8 %collective-permute-start = (bf16[512,128]{1,0:T(8,128)(2,1)}, bf16[512,128]{1,0:T(8,128)(2,1)S(1)}, u32[]{:S(2)}, u32[]{:S(2)}) collective-permute-start(bf16[512,128]{1,0:T(8,128)(2,1)} %refs_0_.1), channel_id=1, source_target_pairs={{0,1},{1,0},{2,3},{3,2},{4,5},{5,4},{6,7},{7,6},{8,9},{9,8},{10,11... | collective-permute-start | bytes 393224 | tf_op jit(solution)/shard_map/ppermute | solution.py:149
  9.5 5.8 %collective-permute-start.8 = (bf16[256,128]{1,0:T(8,128)(2,1)S(1)}, bf16[256,128]{1,0:T(8,128)(2,1)S(1)}, u32[]{:S(2)}, u32[]{:S(2)}) collective-permute-start(bf16[256,128]{1,0:T(8,128)(2,1)S(1)} %get-tuple-element.11), channel_id=1, source_target_pairs={{0,16},{8,24},{16,0},{24,8},{1,17},{9,25},{17,1},{25,9},{2,18},{10... | collective-permute-start | bytes 196616 | tf_op jit(solution)/shard_map/ppermute | solution.py:154
  11.8 6.7 %collective-permute-start.2 = (bf16[512,128]{1,0:T(8,128)(2,1)S(1)}, bf16[512,128]{1,0:T(8,128)(2,1)S(1)}, u32[]{:S(2)}, u32[]{:S(2)}) collective-permute-start(bf16[512,128]{1,0:T(8,128)(2,1)S(1)} %collective-permute-done.1.refs_2_), channel_id=1, source_target_pairs={{0,1},{1,0},{2,3},{3,2},{4,5},{5,4},{6,7},{7,6},{8,9},{9,8},{10,11... | collective-permute-start | bytes 393224 | tf_op jit(solution)/shard_map/ppermute | solution.py:149
  14.8 3.7 %collective-permute-start.4 = (bf16[512,128]{1,0:T(8,128)(2,1)S(1)}, bf16[512,128]{1,0:T(8,128)(2,1)S(1)}, u32[]{:S(2)}, u32[]{:S(2)}) collective-permute-start(bf16[512,128]{1,0:T(8,128)(2,1)S(1)} %collective-permute-done.3.refs_4_), channel_id=1, source_target_pairs={{0,1},{1,0},{2,3},{3,2},{4,5},{5,4},{6,7},{7,6},{8,9},{9,8},{10,11... | collective-permute-start | bytes 393224 | tf_op jit(solution)/shard_map/ppermute | solution.py:149
  14.8 3.6 %collective-permute-start.6 = (bf16[512,128]{1,0:T(8,128)(2,1)S(1)}, bf16[512,128]{1,0:T(8,128)(2,1)S(1)}, u32[]{:S(2)}, u32[]{:S(2)}) collective-permute-start(bf16[512,128]{1,0:T(8,128)(2,1)S(1)} %collective-permute-done.5.refs_6_), channel_id=1, source_target_pairs={{0,1},{1,0},{2,3},{3,2},{4,5},{5,4},{6,7},{7,6},{8,9},{9,8},{10,11... | collective-permute-start | bytes 393224 | tf_op jit(solution)/shard_map/ppermute | solution.py:149
  15.3 3.2 %copy-start = (bf16[512,1024]{1,0:T(8,128)(2,1)S(1)}, bf16[512,1024]{1,0:T(8,128)(2,1)}, u32[]{:S(2)}) copy-start(bf16[512,1024]{1,0:T(8,128)(2,1)} %bound_ref.2) | copy-start | bytes 3145732
  15.3 3.2 %copy-start.4 = (bf16[512,128]{1,0:T(8,128)(2,1)S(1)}, bf16[512,128]{1,0:T(8,128)(2,1)}, u32[]{:S(2)}) copy-start(bf16[512,128]{1,0:T(8,128)(2,1)} %refs_0_.1) | copy-start | bytes 393220
  15.3 3.2 %copy-start.13 = (s32[1,1,4]{2,1,0:T(1,128)S(1)}, s32[1,1,4]{2,1,0:T(1,128)}, u32[]{:S(2)}) copy-start(s32[1,1,4]{2,1,0:T(1,128)} %cols_ref.3) | copy-start | bytes 52
  15.3 3.2 %collective-permute-start.9 = (bf16[256,128]{1,0:T(8,128)(2,1)S(1)}, bf16[256,128]{1,0:T(8,128)(2,1)S(1)}, u32[]{:S(2)}, u32[]{:S(2)}) collective-permute-start(bf16[256,128]{1,0:T(8,128)(2,1)S(1)} %get-tuple-element.12), channel_id=1, source_target_pairs={{0,24},{8,0},{16,8},{24,16},{1,25},{9,1},{17,9},{25,17},{2,26},{10... | collective-permute-start | bytes 196616 | tf_op jit(solution)/shard_map/ppermute | solution.py:154
  18.5 4.4 %copy-start.5 = (bf16[512,512]{1,0:T(8,128)(2,1)S(1)}, bf16[512,512]{1,0:T(8,128)(2,1)}, u32[]{:S(2)}) copy-start(bf16[512,512]{1,0:T(8,128)(2,1)} %panel_ref.3) | copy-start | bytes 1572868
  18.5 4.4 %copy-start.8 = (s32[2,1,1,4,2]{3,4,2,1,0:T(2,128)S(1)}, s32[2,1,1,4,2]{3,4,2,1,0:T(2,128)}, u32[]{:S(2)}) copy-start(s32[2,1,1,4,2]{3,4,2,1,0:T(2,128)} %param.18) | copy-start | bytes 196
  18.5 4.4 %copy-start.10 = (s32[2,1,1,4]{3,2,1,0:T(1,128)S(1)}, s32[2,1,1,4]{3,2,1,0:T(1,128)}, u32[]{:S(2)}) copy-start(s32[2,1,1,4]{3,2,1,0:T(1,128)} %counts_ref.3) | copy-start | bytes 100
  18.5 18.2 %copy-start.6 = (bf16[128,512]{1,0:T(8,128)(2,1)S(1)}, bf16[128,512]{1,0:T(8,128)(2,1)}, u32[]{:S(2)}) copy-start(bf16[128,512]{1,0:T(8,128)(2,1)} %w_ref.2) | copy-start | bytes 393220
  18.6 18.2 %copy-start.12 = (f32[512]{0:T(512)S(1)}, f32[512]{0:T(512)}, u32[]{:S(2)}) copy-start(f32[512]{0:T(512)} %param.21) | copy-start | bytes 6148
  20.2 36.6 %copy-start.1 = (bf16[512,1024]{1,0:T(8,128)(2,1)S(1)}, bf16[512,1024]{1,0:T(8,128)(2,1)}, u32[]{:S(2)}) copy-start(bf16[512,1024]{1,0:T(8,128)(2,1)} %bound_ref.3) | copy-start | bytes 3145732
  20.2 36.6 %copy-start.2 = (bf16[512,512]{1,0:T(8,128)(2,1)S(1)}, bf16[512,512]{1,0:T(8,128)(2,1)}, u32[]{:S(2)}) copy-start(bf16[512,512]{1,0:T(8,128)(2,1)} %w_ref.3) | copy-start | bytes 1572868
  20.2 36.6 %copy-start.11 = (f32[512]{0:T(512)S(1)}, f32[512]{0:T(512)}, u32[]{:S(2)}) copy-start(f32[512]{0:T(512)} %param.23) | copy-start | bytes 6148
  20.2 7.6 %collective-permute-start.11 = (bf16[512,128]{1,0:T(8,128)(2,1)S(1)}, bf16[512,128]{1,0:T(8,128)(2,1)S(1)}, u32[]{:S(2)}, u32[]{:S(2)}) collective-permute-start(bf16[512,128]{1,0:T(8,128)(2,1)S(1)} %first.1.refs_0_), channel_id=1, source_target_pairs={{0,2},{1,3},{2,0},{3,1},{4,6},{5,7},{6,4},{7,5},{8,10},{9,11},{10,... | collective-permute-start | bytes 393224 | tf_op jit(solution)/shard_map/ppermute | solution.py:149
  20.5 9.3 %collective-permute-start.13 = (bf16[512,128]{1,0:T(8,128)(2,1)S(1)}, bf16[512,128]{1,0:T(8,128)(2,1)S(1)}, u32[]{:S(2)}, u32[]{:S(2)}) collective-permute-start(bf16[512,128]{1,0:T(8,128)(2,1)S(1)} %first.1.refs_0_), channel_id=1, source_target_pairs={{0,4},{1,5},{2,6},{3,7},{4,0},{5,1},{6,2},{7,3},{8,12},{9,13},{10,... | collective-permute-start | bytes 393224 | tf_op jit(solution)/shard_map/ppermute | solution.py:149
  20.8 12.3 %collective-permute-start.15 = (bf16[512,128]{1,0:T(8,128)(2,1)S(1)}, bf16[512,128]{1,0:T(8,128)(2,1)S(1)}, u32[]{:S(2)}, u32[]{:S(2)}) collective-permute-start(bf16[512,128]{1,0:T(8,128)(2,1)S(1)} %first.1.refs_0_), channel_id=1, source_target_pairs={{0,6},{1,7},{2,4},{3,5},{4,2},{5,3},{6,0},{7,1},{8,14},{9,15},{10,... | collective-permute-start | bytes 393224 | tf_op jit(solution)/shard_map/ppermute | solution.py:149
  23.6 10.9 %collective-permute-start.10 = (bf16[512,128]{1,0:T(8,128)(2,1)S(1)}, bf16[512,128]{1,0:T(8,128)(2,1)S(1)}, u32[]{:S(2)}, u32[]{:S(2)}) collective-permute-start(bf16[512,128]{1,0:T(8,128)(2,1)S(1)} %first.1.refs_0_), channel_id=1, source_target_pairs={{0,1},{1,0},{2,3},{3,2},{4,5},{5,4},{6,7},{7,6},{8,9},{9,8},{10,11... | collective-permute-start | bytes 393224 | tf_op jit(solution)/shard_map/ppermute | solution.py:149
  27.8 7.6 %collective-permute-start.12 = (bf16[512,128]{1,0:T(8,128)(2,1)S(1)}, bf16[512,128]{1,0:T(8,128)(2,1)S(1)}, u32[]{:S(2)}, u32[]{:S(2)}) collective-permute-start(bf16[512,128]{1,0:T(8,128)(2,1)S(1)} %collective-permute-done.11.refs_2_), channel_id=1, source_target_pairs={{0,1},{1,0},{2,3},{3,2},{4,5},{5,4},{6,7},{7,6},{8,9},{9,8},{10,11... | collective-permute-start | bytes 393224 | tf_op jit(solution)/shard_map/ppermute | solution.py:149
  28.5 11.0 %collective-permute-start.17 = (bf16[256,512]{1,0:T(8,128)(2,1)S(1)}, bf16[256,512]{1,0:T(8,128)(2,1)S(1)}, u32[]{:S(2)}, u32[]{:S(2)}) collective-permute-start(bf16[256,512]{1,0:T(8,128)(2,1)S(1)} %get-tuple-element.15), channel_id=1, source_target_pairs={{0,8},{8,16},{16,24},{24,0},{1,9},{9,17},{17,25},{25,1},{2,10},{10... | collective-permute-start | bytes 786440 | tf_op jit(solution)/shard_map/ppermute | solution.py:154
  29.8 22.5 %collective-permute-start.18 = (bf16[256,512]{1,0:T(8,128)(2,1)S(1)}, bf16[256,512]{1,0:T(8,128)(2,1)S(1)}, u32[]{:S(2)}, u32[]{:S(2)}) collective-permute-start(bf16[256,512]{1,0:T(8,128)(2,1)S(1)} %get-tuple-element.16), channel_id=1, source_target_pairs={{0,16},{8,24},{16,0},{24,8},{1,17},{9,25},{17,1},{25,9},{2,18},{10... | collective-permute-start | bytes 786440 | tf_op jit(solution)/shard_map/ppermute | solution.py:154
  33.1 23.7 %collective-permute-start.19 = (bf16[256,512]{1,0:T(8,128)(2,1)S(1)}, bf16[256,512]{1,0:T(8,128)(2,1)S(1)}, u32[]{:S(2)}, u32[]{:S(2)}) collective-permute-start(bf16[256,512]{1,0:T(8,128)(2,1)S(1)} %get-tuple-element.17), channel_id=1, source_target_pairs={{0,24},{8,0},{16,8},{24,16},{1,25},{9,1},{17,9},{25,17},{2,26},{10... | collective-permute-start | bytes 786440 | tf_op jit(solution)/shard_map/ppermute | solution.py:154
  34.6 1.8 %collective-permute-start.14 = (bf16[512,128]{1,0:T(8,128)(2,1)S(1)}, bf16[512,128]{1,0:T(8,128)(2,1)S(1)}, u32[]{:S(2)}, u32[]{:S(2)}) collective-permute-start(bf16[512,128]{1,0:T(8,128)(2,1)S(1)} %collective-permute-done.13.refs_4_), channel_id=1, source_target_pairs={{0,1},{1,0},{2,3},{3,2},{4,5},{5,4},{6,7},{7,6},{8,9},{9,8},{10,11... | collective-permute-start | bytes 393224 | tf_op jit(solution)/shard_map/ppermute | solution.py:149
  35.4 1.3 %collective-permute-start.16 = (bf16[512,128]{1,0:T(8,128)(2,1)S(1)}, bf16[512,128]{1,0:T(8,128)(2,1)S(1)}, u32[]{:S(2)}, u32[]{:S(2)}) collective-permute-start(bf16[512,128]{1,0:T(8,128)(2,1)S(1)} %collective-permute-done.15.refs_6_), channel_id=1, source_target_pairs={{0,1},{1,0},{2,3},{3,2},{4,5},{5,4},{6,7},{7,6},{8,9},{9,8},{10,11... | collective-permute-start | bytes 393224 | tf_op jit(solution)/shard_map/ppermute | solution.py:149
where the time goes:
time: 58.7 us; the launch traced here: 58.4 us
  starting transfers between devices  26.4 us (45%)
  waiting for transfers between devices  19.5 us (33%)
  Pallas kernels  7.3 us (12%)
  local copies, waits for them, and re-layouts  4.45 us (8%)
  between operations  0.8 us (1%)
    ppermute x6, waiting for transfers between devices, send_on(): lax.ppermute(block, 'dom', [(i, (i + shift) % n_dom) for i in range(n_dom)])  18.2 us
    ppermute x14, starting transfers between devices, swap(): return lax.ppermute(block, 'blk', [(i, i ^ apart) for i in range(n_blk)])  16.4 us
    ppermute x6, starting transfers between devices, send_on(): lax.ppermute(block, 'dom', [(i, (i + shift) % n_dom) for i in range(n_dom)])  10 us
    unnamed x29, local copies, waits for them, and re-layouts  4.45 us
    pallas_call x1, Pallas kernels, inside(): pl.pallas_call(functools.partial(inside_kernel, len(panels)), out_shape=[...  2.68 us
    pallas_call x1, Pallas kernels, last_layer(): pl.pallas_call(last_kernel, out_shape=jax.ShapeDtypeStruct((total.shape[0...  1.64 us
    pallas_call x1, Pallas kernels, first_layer(): pl.pallas_call(functools.partial(first_kernel, len(panels)), out_shape=pl...  1.6 us
    pallas_call x2, Pallas kernels, pack(): pl.pallas_call(functools.partial(pack_kernel, layer), out_shape=[pltpu.VM...  1.38 us
  transfers between devices with their start and end apart: 20, of which 5 were waited for; matrix products, arithmetic and copies ran while one was open for 4% of the time, Pallas kernels for 7%

commit v1 on v0

--- a/solution.py
+++ b/solution.py
@@ -15,6 +15,10 @@
 SMEM = pl.BlockSpec(memory_space=pltpu.SMEM)
 
 
+def far(array):
+    return pltpu.with_memory_space_constraint(array, pltpu.HBM)
+
+
 def near(array):
     return pltpu.with_memory_space_constraint(array, pltpu.VMEM)
 
@@ -23,35 +27,52 @@
     return jnp.dot(a, b, preferred_element_type=F32)
 
 
-def pack_kernel(layer, ids_ref, counts_ref, panel_ref, *out_refs):
-    slots, n_dom = ids_ref.shape[-2:]
-    rows = out_refs[0].shape[0] // slots
+def pack_kernel(*refs):
+    layers, slots, n_dom = refs[0].shape[0], *refs[0].shape[-2:]
+    came_refs = refs[:layers + 2]
+    out_refs = refs[layers + 2:-layers - 3]
+    held_refs, sems = refs[-layers - 3:-1], refs[-1]
+    ids_ref, counts_ref, *panel_refs = held_refs
+    copies = [pltpu.make_async_copy(*pair, sems.at[n]) for n, pair in enumerate(zip(came_refs, held_refs))]
+    for copy in copies:
+        copy.start()
+    copies[0].wait()
+    copies[1].wait()
     dom = lax.axis_index("dom")
-    for shift, out_ref in enumerate(out_refs, 1):
-        reader = lax.rem(dom + shift, n_dom)
-        live = counts_ref[layer, 0, 0, reader]
-        for slot in range(slots):
-            start = pl.multiple_of(ids_ref[layer, 0, 0, slot, reader] * rows, rows)
-            here = pl.ds(slot * rows, rows)
-
-            @pl.when(slot < live)
-            def _():
-                out_ref[here, :] = panel_ref[pl.ds(start, rows), :]
-
-            @pl.when(slot >= live)
-            def _():
-                out_ref[here, :] = jnp.zeros((rows, out_ref.shape[1]), out_ref.dtype)
-
-
-def pack(layer, ids, counts, panel, slot_rows):
+    for layer in range(layers):
+        copies[2 + layer].wait()
+        for apart in range(1, n_dom):
+            out_ref = out_refs[layer * (n_dom - 1) + apart - 1]
+            rows, width = out_ref.shape[0] // slots, out_ref.shape[1]
+            reader = lax.bitwise_xor(dom, apart)
+            live = counts_ref[layer, 0, 0, reader]
+            for slot in range(slots):
+                start = pl.multiple_of(ids_ref[layer, 0, 0, slot, reader] * rows, rows)
+                here = pl.ds(slot * rows, rows)
+
+                @pl.when(slot < live)
+                def _():
+                    out_ref[here, :] = panel_refs[layer][pl.ds(start, rows), :]
+
+                @pl.when(slot >= live)
+                def _():
+                    out_ref[here, :] = jnp.zeros((rows, width), out_ref.dtype)
+
+
+def pack(ids, counts, panels, slot_rows):
     n_dom = ids.shape[-1]
-    return pl.pallas_call(
-        functools.partial(pack_kernel, layer),
-        out_shape=[pltpu.VMEM((slot_rows, panel.shape[1]), panel.dtype)] * (n_dom - 1),
-        in_specs=[SMEM, SMEM, VMEM],
-        out_specs=[VMEM] * (n_dom - 1),
-        compiler_params=pltpu.CompilerParams(vmem_limit_bytes=MIB),
-    )(ids, counts, near(panel))
+    blocks = pl.pallas_call(
+        pack_kernel,
+        out_shape=[pltpu.VMEM((slot_rows, panel.shape[1]), panel.dtype) for panel in panels for _ in range(n_dom - 1)],
+        in_specs=[pl.BlockSpec(memory_space=pltpu.HBM)] * (2 + len(panels)),
+        out_specs=[VMEM] * (len(panels) * (n_dom - 1)),
+        scratch_shapes=[pltpu.SMEM(a.shape, a.dtype) for a in (ids, counts)]
+        + [pltpu.VMEM(panel.shape, panel.dtype) for panel in panels]
+        + [pltpu.SemaphoreType.DMA((2 + len(panels),))],
+        compiler_params=pltpu.CompilerParams(vmem_limit_bytes=2 * MIB),
+        name="pack",
+    )(*map(far, (ids, counts, *panels)))
+    return [blocks[n * (n_dom - 1):(n + 1) * (n_dom - 1)] for n in range(len(panels))]
 
 
 def pick_panels(blk, cols_ref, panel_refs, chosen_ref):
@@ -65,12 +86,11 @@
                 chosen_ref[k] = panel_ref[...]
 
 
-def border_product(dom, bound_ref, border_refs, shifts):
-    n_dom = bound_ref.shape[1] // border_refs[0].shape[0]
+def border_product(dom, bound_ref, border_refs, distances):
     total = None
-    for border_ref, shift in zip(border_refs, shifts):
+    for border_ref, apart in zip(border_refs, distances):
         width = border_ref.shape[0]
-        owner = lax.rem(dom + n_dom - shift, n_dom)
+        owner = lax.bitwise_xor(dom, apart)
         part = dot(bound_ref[:, pl.ds(pl.multiple_of(owner * width, width), width)], border_ref[...])
         total = part if total is None else total + part
     return total
@@ -144,14 +164,8 @@
     )(*map(near, (total, bound, w_out, b_out, *border)))
 
 
-def swap(block, apart):
-    n_blk = lax.axis_size("blk")
-    return lax.ppermute(block, "blk", [(i, i ^ apart) for i in range(n_blk)])
-
-
-def send_on(block, shift):
-    n_dom = lax.axis_size("dom")
-    return lax.ppermute(block, "dom", [(i, (i + shift) % n_dom) for i in range(n_dom)])
+def swap(block, axis, apart):
+    return lax.ppermute(block, axis, [(i, i ^ apart) for i in range(lax.axis_size(axis))])
 
 
 def all_panels(panel):
@@ -159,24 +173,24 @@
     panels = {0: panel}
     far = sorted(range(2, n_blk, 2), key=lambda d: -bin(d).count("1"))
     for d in far:
-        panels[d] = swap(panel, d)
-    panels[1] = swap(panel, 1)
+        panels[d] = swap(panel, "blk", d)
+    panels[1] = swap(panel, "blk", 1)
     for d in far:
-        panels[d + 1] = swap(panels[d], 1)
+        panels[d + 1] = swap(panels[d], "blk", 1)
     return [panels[d] for d in range(n_blk)]
 
 
-def borders(layer, ids, counts, panel, slot_rows):
-    blocks = pack(layer, ids, counts, panel, slot_rows)
-    return [send_on(block, s) for s, block in enumerate(blocks, 1)]
+def borders(blocks):
+    return [swap(block, "dom", apart) for apart, block in enumerate(blocks, 1)]
 
 
 def body(features, history, adj_tiles, tile_cols, bound_one, bound_two, block_ids, block_counts, w_in, b_in, w_out, b_out):
     slot_rows = bound_one.shape[1] // lax.axis_size("dom")
     ids = block_ids.swapaxes(3, 4)
+    out_one, out_two = pack(ids, block_counts, (features, history), slot_rows)
+    border_one = borders(out_one)
     panels_one = all_panels(features)
-    border_one = borders(0, ids, block_counts, features, slot_rows)
-    border_two = borders(1, ids, block_counts, history, slot_rows)
+    border_two = borders(out_two)
     tiles = adj_tiles.transpose(1, 0, 2)
     agg = first_layer(tile_cols, tiles, bound_one, panels_one, border_one)
     panels_two = all_panels(agg)

time: 58.7 us -> 58.6 us (level)
  the two profiles are of different devices: /device:TPU:15 before, /device:TPU:12 now
where the time goes in v1:
time: 58.6 us; the launch traced here: 58.4 us
  waiting for transfers between devices  29.4 us (50%)
  starting transfers between devices  19 us (32%)
  Pallas kernels  7.18 us (12%)
  local copies, waits for them, and re-layouts  2.04 us (3%)
  between operations  0.78 us (1%)
    ppermute x20, waiting for transfers between devices, swap(): lax.ppermute(block, axis, [(i, i ^ apart) for i in range(lax.axis_size(ax...  29.4 us
    ppermute x20, starting transfers between devices, swap(): lax.ppermute(block, axis, [(i, i ^ apart) for i in range(lax.axis_size(ax...  19 us
    pallas_call x1, Pallas kernels, inside(): pl.pallas_call(functools.partial(inside_kernel, len(panels)), out_shape=[...  2.68 us
    unnamed x17, local copies, waits for them, and re-layouts  2.04 us
    pallas_call x1, Pallas kernels, last_layer(): pl.pallas_call(last_kernel, out_shape=jax.ShapeDtypeStruct((total.shape[0...  1.66 us
    pallas_call x1, Pallas kernels, first_layer(): pl.pallas_call(functools.partial(first_kernel, len(panels)), out_shape=pl...  1.6 us
    pallas_call x1, Pallas kernels, pack(): pl.pallas_call(pack_kernel, out_shape=[pltpu.VMEM((slot_rows, panel.shape...  1.23 us
  transfers between devices with their start and end apart: 20, of which 9 were waited for; matrix products, arithmetic and copies ran while one was open for 3% of the time, Pallas kernels for 7%

profile of v1, /device:TPU:12, one launch (start us, length us, event | category | flops | bytes accessed | tf_op | source)
XLA Modules:
  0.0 58.4 jit_solution(15327366200032264183)
XLA Ops:
  0.6 1.5 %collective-permute-start.5 = (bf16[512,128]{1,0:T(8,128)(2,1)}, bf16[512,128]{1,0:T(8,128)(2,1)S(1)}, u32[]{:S(2)}, u32[]{:S(2)}) collective-permute-start(bf16[512,128]{1,0:T(8,128)(2,1)} %refs_0_.1), channel_id=1, source_target_pairs={{0,6},{1,7},{2,4},{3,5},{4,2},{5,3},{6,0},{7,1},{8,14},{9,15},{10,... | collective-permute-start | bytes 393224 | tf_op jit(solution)/shard_map/ppermute | solution.py:168
  2.1 1.5 %collective-permute-start.3 = (bf16[512,128]{1,0:T(8,128)(2,1)}, bf16[512,128]{1,0:T(8,128)(2,1)S(1)}, u32[]{:S(2)}, u32[]{:S(2)}) collective-permute-start(bf16[512,128]{1,0:T(8,128)(2,1)} %refs_0_.1), channel_id=1, source_target_pairs={{0,4},{1,5},{2,6},{3,7},{4,0},{5,1},{6,2},{7,3},{8,12},{9,13},{10,... | collective-permute-start | bytes 393224 | tf_op jit(solution)/shard_map/ppermute | solution.py:168
  3.6 0.5 collective-permute-start.1
  4.2 1.2 %pack.1 = (bf16[256,128]{1,0:T(8,128)(2,1)S(1)}, bf16[256,128]{1,0:T(8,128)(2,1)S(1)}, bf16[256,128]{1,0:T(8,128)(2,1)S(1)}, bf16[256,512]{1,0:T(8,128)(2,1)S(1)...) custom-call(s32[2,1,1,2,4]{4,3,2,1,0:T(2,128)} %bitcast.10, s32[2,1,1,4]{3,2,1,0:T(1,128)} %refs_1_.1, ...), custom_call_target="tpu_custom_call" | custom-call | tf_op jit(solution)/shard_map/pack/pallas_call | solution.py:64
  5.4 0.5 collective-permute-start.7
  5.9 0.0 collective-permute-start
  5.9 3.8 %collective-permute-done.7.refs_8_ = bf16[256,128]{1,0:T(8,128)(2,1)S(1)} collective-permute-done((bf16[256,128]{1,0:T(8,128)(2,1)S(1)}, bf16[256,128]{1,0:T(8,128)(2,1)S(1)}, u32[]{:S(2)}, u32[]{:S(2)}) %collective-permute-start.7) | collective-permute-done | bytes 65568 | tf_op jit(solution)/shard_map/ppermute | solution.py:168
  9.8 2.6 %collective-permute-start.8 = (bf16[256,128]{1,0:T(8,128)(2,1)S(1)}, bf16[256,128]{1,0:T(8,128)(2,1)S(1)}, u32[]{:S(2)}, u32[]{:S(2)}) collective-permute-start(bf16[256,128]{1,0:T(8,128)(2,1)S(1)} %get-tuple-element.11), channel_id=1, source_target_pairs={{0,16},{8,24},{16,0},{24,8},{1,17},{9,25},{17,1},{25,9},{2,18},{10... | collective-permute-start | bytes 196616 | tf_op jit(solution)/shard_map/ppermute | solution.py:168
  12.3 0.0 collective-permute-done.5.refs_6_
  12.3 0.0 collective-permute-start.6
  12.3 0.0 collective-permute-done.3.refs_4_
  12.4 0.5 collective-permute-start.4
  12.9 0.0 collective-permute-done.1.refs_2_
  12.9 0.1 collective-permute-start.2
  12.9 2.4 %collective-permute-done.8.refs_9_ = bf16[256,128]{1,0:T(8,128)(2,1)S(1)} collective-permute-done((bf16[256,128]{1,0:T(8,128)(2,1)S(1)}, bf16[256,128]{1,0:T(8,128)(2,1)S(1)}, u32[]{:S(2)}, u32[]{:S(2)}) %collective-permute-start.8) | collective-permute-done | bytes 65568 | tf_op jit(solution)/shard_map/ppermute | solution.py:168
  15.4 0.0 copy-start
  15.4 0.0 copy-start.3
  15.4 0.0 copy-start.7
  15.4 1.2 %collective-permute-start.9 = (bf16[256,128]{1,0:T(8,128)(2,1)S(1)}, bf16[256,128]{1,0:T(8,128)(2,1)S(1)}, u32[]{:S(2)}, u32[]{:S(2)}) collective-permute-start(bf16[256,128]{1,0:T(8,128)(2,1)S(1)} %get-tuple-element.12), channel_id=1, source_target_pairs={{0,24},{8,16},{16,8},{24,0},{1,25},{9,17},{17,9},{25,1},{2,26},{10... | collective-permute-start | bytes 196616 | tf_op jit(solution)/shard_map/ppermute | solution.py:168
  16.6 2.0 %copy.16 = bf16[512,4,512]{2,0,1:T(8,128)(2,1)S(1)} copy(bf16[512,4,512]{2,1,0:T(4,128)(2,1)} %param.14) | data formatting | bytes 4194304 | tf_op args[2]
  18.6 1.1 %collective-permute-done.9.refs_10_ = bf16[256,128]{1,0:T(8,128)(2,1)S(1)} collective-permute-done((bf16[256,128]{1,0:T(8,128)(2,1)S(1)}, bf16[256,128]{1,0:T(8,128)(2,1)S(1)}, u32[]{:S(2)}, u32[]{:S(2)}) %collective-permute-start.9) | collective-permute-done | bytes 65568 | tf_op jit(solution)/shard_map/ppermute | solution.py:168
  19.7 0.0 collective-permute-done.refs_1_
  19.7 0.0 collective-permute-done.6.refs_7_
  19.7 0.0 collective-permute-done.4.refs_5_
  19.7 0.0 collective-permute-done.2.refs_3_
  19.7 0.0 copy-done
  19.7 0.0 copy-done.3
  19.7 0.0 copy-done.7
  19.7 0.0 copy-start.4
  19.7 0.0 copy-start.6
  19.7 1.6 %first.1.refs_0_ = bf16[512,128]{1,0:T(8,128)(2,1)S(1)} custom-call(s32[1,1,4]{2,1,0:T(1,128)S(1)} %copy-done.7, bf16[4,512,512]{2,1,0:T(8,128)(2,1)S(1)} %bitcast.6, bf16[512,1024]{1,0:T(8,128)(2,1)S(1)} %copy-done, bf16[512,128]{1,0:T(8,128)(2,1)S(1)} %copy-done.3, bf16[512,128]{1,0:T(8,128)(2,1)S(1)} %collective-permute-done.refs_1_, ...), custom_call_target="tpu_custom_call" | custom-call | tf_op jit(solution)/shard_map/first/pallas_call | solution.py:111
  21.3 0.0 copy-start.1
  21.4 0.0 copy-start.2
  21.4 0.0 copy-start.5
  21.4 1.5 %collective-permute-start.15 = (bf16[512,128]{1,0:T(8,128)(2,1)S(1)}, bf16[512,128]{1,0:T(8,128)(2,1)S(1)}, u32[]{:S(2)}, u32[]{:S(2)}) collective-permute-start(bf16[512,128]{1,0:T(8,128)(2,1)S(1)} %first.1.refs_0_), channel_id=1, source_target_pairs={{0,6},{1,7},{2,4},{3,5},{4,2},{5,3},{6,0},{7,1},{8,14},{9,15},{10,... | collective-permute-start | bytes 393224 | tf_op jit(solution)/shard_map/ppermute | solution.py:168
  22.9 1.5 %collective-permute-start.13 = (bf16[512,128]{1,0:T(8,128)(2,1)S(1)}, bf16[512,128]{1,0:T(8,128)(2,1)S(1)}, u32[]{:S(2)}, u32[]{:S(2)}) collective-permute-start(bf16[512,128]{1,0:T(8,128)(2,1)S(1)} %first.1.refs_0_), channel_id=1, source_target_pairs={{0,4},{1,5},{2,6},{3,7},{4,0},{5,1},{6,2},{7,3},{8,12},{9,13},{10,... | collective-permute-start | bytes 393224 | tf_op jit(solution)/shard_map/ppermute | solution.py:168
  24.4 0.6 collective-permute-start.11
  24.9 0.0 collective-permute-start.10
  24.9 2.5 %collective-permute-done.15.refs_6_ = bf16[512,128]{1,0:T(8,128)(2,1)S(1)} collective-permute-done((bf16[512,128]{1,0:T(8,128)(2,1)S(1)}, bf16[512,128]{1,0:T(8,128)(2,1)S(1)}, u32[]{:S(2)}, u32[]{:S(2)}) %collective-permute-start.15) | collective-permute-done | bytes 131104 | tf_op jit(solution)/shard_map/ppermute | solution.py:168
  27.4 0.0 collective-permute-start.16
  27.4 2.8 %collective-permute-start.17 = (bf16[256,512]{1,0:T(8,128)(2,1)S(1)}, bf16[256,512]{1,0:T(8,128)(2,1)S(1)}, u32[]{:S(2)}, u32[]{:S(2)}) collective-permute-start(bf16[256,512]{1,0:T(8,128)(2,1)S(1)} %get-tuple-element.15), channel_id=1, source_target_pairs={{0,8},{8,0},{16,24},{24,16},{1,9},{9,1},{17,25},{25,17},{2,10},{10... | collective-permute-start | bytes 786440 | tf_op jit(solution)/shard_map/ppermute | solution.py:168
  30.2 0.0 collective-permute-done.13.refs_4_
  30.2 3.7 %collective-permute-start.18 = (bf16[256,512]{1,0:T(8,128)(2,1)S(1)}, bf16[256,512]{1,0:T(8,128)(2,1)S(1)}, u32[]{:S(2)}, u32[]{:S(2)}) collective-permute-start(bf16[256,512]{1,0:T(8,128)(2,1)S(1)} %get-tuple-element.16), channel_id=1, source_target_pairs={{0,16},{8,24},{16,0},{24,8},{1,17},{9,25},{17,1},{25,9},{2,18},{10... | collective-permute-start | bytes 786440 | tf_op jit(solution)/shard_map/ppermute | solution.py:168
  33.9 0.0 collective-permute-done.11.refs_2_
  33.9 0.0 collective-permute-start.19
  33.9 0.0 collective-permute-done.10.refs_1_
  33.9 0.1 collective-permute-start.14
  34.0 0.0 collective-permute-done.16.refs_7_
  34.0 0.5 collective-permute-start.12
  34.5 0.8 %collective-permute-done.14.refs_5_ = bf16[512,128]{1,0:T(8,128)(2,1)S(1)} collective-permute-done((bf16[512,128]{1,0:T(8,128)(2,1)S(1)}, bf16[512,128]{1,0:T(8,128)(2,1)S(1)}, u32[]{:S(2)}, u32[]{:S(2)}) %collective-permute-start.14) | collective-permute-done | bytes 131104 | tf_op jit(solution)/shard_map/ppermute | solution.py:168
  35.3 0.2 collective-permute-done.12.refs_3_
  35.5 0.0 copy-done.4
  35.5 0.0 copy-done.6
  35.5 2.7 %inside.1 = (bf16[512,512]{1,0:T(8,128)(2,1)}, f32[512,512]{1,0:T(8,128)S(1)}) custom-call(s32[1,1,4]{2,1,0:T(1,128)S(1)} %copy-done.7, bf16[4,512,512]{2,1,0:T(8,128)(2,1)S(1)} %bitcast.7, bf16[128,512]{1,0:T(8,128)(2,1)S(1)} %copy-done.4, f32[1,512]{1,0:T(1,128)S(1)} %bitcast.9, bf16[512,128]{1,0:T(8,128)(2,1)S(1)} %first.1.refs_0_, ...), custom_call_target="tpu_custom_call" | custom-call | tf_op jit(solution)/shard_map/inside/pallas_call | solution.py:139
  38.2 3.5 %collective-permute-done.17.refs_0_ = bf16[256,512]{1,0:T(8,128)(2,1)S(1)} collective-permute-done((bf16[256,512]{1,0:T(8,128)(2,1)S(1)}, bf16[256,512]{1,0:T(8,128)(2,1)S(1)}, u32[]{:S(2)}, u32[]{:S(2)}) %collective-permute-start.17) | collective-permute-done | bytes 262176 | tf_op jit(solution)/shard_map/ppermute | solution.py:168
  41.7 10.1 %collective-permute-done.18.refs_1_ = bf16[256,512]{1,0:T(8,128)(2,1)S(1)} collective-permute-done((bf16[256,512]{1,0:T(8,128)(2,1)S(1)}, bf16[256,512]{1,0:T(8,128)(2,1)S(1)}, u32[]{:S(2)}, u32[]{:S(2)}) %collective-permute-start.18) | collective-permute-done | bytes 262176 | tf_op jit(solution)/shard_map/ppermute | solution.py:168
  51.8 4.9 %collective-permute-done.19.refs_2_ = bf16[256,512]{1,0:T(8,128)(2,1)S(1)} collective-permute-done((bf16[256,512]{1,0:T(8,128)(2,1)S(1)}, bf16[256,512]{1,0:T(8,128)(2,1)S(1)}, u32[]{:S(2)}, u32[]{:S(2)}) %collective-permute-start.19) | collective-permute-done | bytes 262176 | tf_op jit(solution)/shard_map/ppermute | solution.py:168
  56.7 0.0 copy-done.1
  56.7 0.0 copy-done.2
  56.7 0.0 copy-done.5
  56.7 1.7 %last.1 = bf16[512,512]{1,0:T(8,128)(2,1)} custom-call(f32[512,512]{1,0:T(8,128)S(1)} %get-tuple-element.14.total_ref, bf16[512,1024]{1,0:T(8,128)(2,1)S(1)} %copy-done.1, bf16[512,512]{1,0:T(8,128)(2,1)S(1)} %copy-done.2, f32[1,512]{1,0:T(1,128)S(1)} %bitcast.8, bf16[256,512]{1,0:T(8,128)(2,1)S(1)} %collective-permute-done.17.refs_0_, ...), custom_call_target="tpu_custom_call" | custom-call | tf_op jit(solution)/shard_map/last/pallas_call | solution.py:157
Async XLA Ops:
  0.6 11.7 %collective-permute-start.5 = (bf16[512,128]{1,0:T(8,128)(2,1)}, bf16[512,128]{1,0:T(8,128)(2,1)S(1)}, u32[]{:S(2)}, u32[]{:S(2)}) collective-permute-start(bf16[512,128]{1,0:T(8,128)(2,1)} %refs_0_.1), channel_id=1, source_target_pairs={{0,6},{1,7},{2,4},{3,5},{4,2},{5,3},{6,0},{7,1},{8,14},{9,15},{10,... | collective-permute-start | bytes 393224 | tf_op jit(solution)/shard_map/ppermute | solution.py:168
  2.1 10.2 %collective-permute-start.3 = (bf16[512,128]{1,0:T(8,128)(2,1)}, bf16[512,128]{1,0:T(8,128)(2,1)S(1)}, u32[]{:S(2)}, u32[]{:S(2)}) collective-permute-start(bf16[512,128]{1,0:T(8,128)(2,1)} %refs_0_.1), channel_id=1, source_target_pairs={{0,4},{1,5},{2,6},{3,7},{4,0},{5,1},{6,2},{7,3},{8,12},{9,13},{10,... | collective-permute-start | bytes 393224 | tf_op jit(solution)/shard_map/ppermute | solution.py:168
  3.6 9.2 %collective-permute-start.1 = (bf16[512,128]{1,0:T(8,128)(2,1)}, bf16[512,128]{1,0:T(8,128)(2,1)S(1)}, u32[]{:S(2)}, u32[]{:S(2)}) collective-permute-start(bf16[512,128]{1,0:T(8,128)(2,1)} %refs_0_.1), channel_id=1, source_target_pairs={{0,2},{1,3},{2,0},{3,1},{4,6},{5,7},{6,4},{7,5},{8,10},{9,11},{10,... | collective-permute-start | bytes 393224 | tf_op jit(solution)/shard_map/ppermute | solution.py:168
  5.4 4.3 %collective-permute-start.7 = (bf16[256,128]{1,0:T(8,128)(2,1)S(1)}, bf16[256,128]{1,0:T(8,128)(2,1)S(1)}, u32[]{:S(2)}, u32[]{:S(2)}) collective-permute-start(bf16[256,128]{1,0:T(8,128)(2,1)S(1)} %get-tuple-element.10), channel_id=1, source_target_pairs={{0,8},{8,0},{16,24},{24,16},{1,9},{9,1},{17,25},{25,17},{2,10},{10... | collective-permute-start | bytes 196616 | tf_op jit(solution)/shard_map/ppermute | solution.py:168
  5.9 13.7 %collective-permute-start = (bf16[512,128]{1,0:T(8,128)(2,1)}, bf16[512,128]{1,0:T(8,128)(2,1)S(1)}, u32[]{:S(2)}, u32[]{:S(2)}) collective-permute-start(bf16[512,128]{1,0:T(8,128)(2,1)} %refs_0_.1), channel_id=1, source_target_pairs={{0,1},{1,0},{2,3},{3,2},{4,5},{5,4},{6,7},{7,6},{8,9},{9,8},{10,11... | collective-permute-start | bytes 393224 | tf_op jit(solution)/shard_map/ppermute | solution.py:168
  9.8 5.6 %collective-permute-start.8 = (bf16[256,128]{1,0:T(8,128)(2,1)S(1)}, bf16[256,128]{1,0:T(8,128)(2,1)S(1)}, u32[]{:S(2)}, u32[]{:S(2)}) collective-permute-start(bf16[256,128]{1,0:T(8,128)(2,1)S(1)} %get-tuple-element.11), channel_id=1, source_target_pairs={{0,16},{8,24},{16,0},{24,8},{1,17},{9,25},{17,1},{25,9},{2,18},{10... | collective-permute-start | bytes 196616 | tf_op jit(solution)/shard_map/ppermute | solution.py:168
  12.3 7.3 %collective-permute-start.6 = (bf16[512,128]{1,0:T(8,128)(2,1)S(1)}, bf16[512,128]{1,0:T(8,128)(2,1)S(1)}, u32[]{:S(2)}, u32[]{:S(2)}) collective-permute-start(bf16[512,128]{1,0:T(8,128)(2,1)S(1)} %collective-permute-done.5.refs_6_), channel_id=1, source_target_pairs={{0,1},{1,0},{2,3},{3,2},{4,5},{5,4},{6,7},{7,6},{8,9},{9,8},{10,11... | collective-permute-start | bytes 393224 | tf_op jit(solution)/shard_map/ppermute | solution.py:168
  12.4 7.3 %collective-permute-start.4 = (bf16[512,128]{1,0:T(8,128)(2,1)S(1)}, bf16[512,128]{1,0:T(8,128)(2,1)S(1)}, u32[]{:S(2)}, u32[]{:S(2)}) collective-permute-start(bf16[512,128]{1,0:T(8,128)(2,1)S(1)} %collective-permute-done.3.refs_4_), channel_id=1, source_target_pairs={{0,1},{1,0},{2,3},{3,2},{4,5},{5,4},{6,7},{7,6},{8,9},{9,8},{10,11... | collective-permute-start | bytes 393224 | tf_op jit(solution)/shard_map/ppermute | solution.py:168
  12.9 6.8 %collective-permute-start.2 = (bf16[512,128]{1,0:T(8,128)(2,1)S(1)}, bf16[512,128]{1,0:T(8,128)(2,1)S(1)}, u32[]{:S(2)}, u32[]{:S(2)}) collective-permute-start(bf16[512,128]{1,0:T(8,128)(2,1)S(1)} %collective-permute-done.1.refs_2_), channel_id=1, source_target_pairs={{0,1},{1,0},{2,3},{3,2},{4,5},{5,4},{6,7},{7,6},{8,9},{9,8},{10,11... | collective-permute-start | bytes 393224 | tf_op jit(solution)/shard_map/ppermute | solution.py:168
  15.4 4.3 %copy-start = (bf16[512,1024]{1,0:T(8,128)(2,1)S(1)}, bf16[512,1024]{1,0:T(8,128)(2,1)}, u32[]{:S(2)}) copy-start(bf16[512,1024]{1,0:T(8,128)(2,1)} %bound_ref.2) | copy-start | bytes 3145732
  15.4 4.3 %copy-start.3 = (bf16[512,128]{1,0:T(8,128)(2,1)S(1)}, bf16[512,128]{1,0:T(8,128)(2,1)}, u32[]{:S(2)}) copy-start(bf16[512,128]{1,0:T(8,128)(2,1)} %refs_0_.1) | copy-start | bytes 393220
  15.4 4.3 %copy-start.7 = (s32[1,1,4]{2,1,0:T(1,128)S(1)}, s32[1,1,4]{2,1,0:T(1,128)}, u32[]{:S(2)}) copy-start(s32[1,1,4]{2,1,0:T(1,128)} %cols_ref.3) | copy-start | bytes 52
  15.4 4.3 %collective-permute-start.9 = (bf16[256,128]{1,0:T(8,128)(2,1)S(1)}, bf16[256,128]{1,0:T(8,128)(2,1)S(1)}, u32[]{:S(2)}, u32[]{:S(2)}) collective-permute-start(bf16[256,128]{1,0:T(8,128)(2,1)S(1)} %get-tuple-element.12), channel_id=1, source_target_pairs={{0,24},{8,16},{16,8},{24,0},{1,25},{9,17},{17,9},{25,1},{2,26},{10... | collective-permute-start | bytes 196616 | tf_op jit(solution)/shard_map/ppermute | solution.py:168
  19.7 15.8 %copy-start.4 = (bf16[128,512]{1,0:T(8,128)(2,1)S(1)}, bf16[128,512]{1,0:T(8,128)(2,1)}, u32[]{:S(2)}) copy-start(bf16[128,512]{1,0:T(8,128)(2,1)} %w_ref.2) | copy-start | bytes 393220
  19.7 15.8 %copy-start.6 = (f32[512]{0:T(512)S(1)}, f32[512]{0:T(512)}, u32[]{:S(2)}) copy-start(f32[512]{0:T(512)} %param.21) | copy-start | bytes 6148
  21.3 35.4 %copy-start.1 = (bf16[512,1024]{1,0:T(8,128)(2,1)S(1)}, bf16[512,1024]{1,0:T(8,128)(2,1)}, u32[]{:S(2)}) copy-start(bf16[512,1024]{1,0:T(8,128)(2,1)} %bound_ref.3) | copy-start | bytes 3145732
  21.4 35.4 %copy-start.2 = (bf16[512,512]{1,0:T(8,128)(2,1)S(1)}, bf16[512,512]{1,0:T(8,128)(2,1)}, u32[]{:S(2)}) copy-start(bf16[512,512]{1,0:T(8,128)(2,1)} %w_ref.3) | copy-start | bytes 1572868
  21.4 35.4 %copy-start.5 = (f32[512]{0:T(512)S(1)}, f32[512]{0:T(512)}, u32[]{:S(2)}) copy-start(f32[512]{0:T(512)} %param.23) | copy-start | bytes 6148
  21.4 6.0 %collective-permute-start.15 = (bf16[512,128]{1,0:T(8,128)(2,1)S(1)}, bf16[512,128]{1,0:T(8,128)(2,1)S(1)}, u32[]{:S(2)}, u32[]{:S(2)}) collective-permute-start(bf16[512,128]{1,0:T(8,128)(2,1)S(1)} %first.1.refs_0_), channel_id=1, source_target_pairs={{0,6},{1,7},{2,4},{3,5},{4,2},{5,3},{6,0},{7,1},{8,14},{9,15},{10,... | collective-permute-start | bytes 393224 | tf_op jit(solution)/shard_map/ppermute | solution.py:168
  22.9 7.4 %collective-permute-start.13 = (bf16[512,128]{1,0:T(8,128)(2,1)S(1)}, bf16[512,128]{1,0:T(8,128)(2,1)S(1)}, u32[]{:S(2)}, u32[]{:S(2)}) collective-permute-start(bf16[512,128]{1,0:T(8,128)(2,1)S(1)} %first.1.refs_0_), channel_id=1, source_target_pairs={{0,4},{1,5},{2,6},{3,7},{4,0},{5,1},{6,2},{7,3},{8,12},{9,13},{10,... | collective-permute-start | bytes 393224 | tf_op jit(solution)/shard_map/ppermute | solution.py:168
  24.4 9.5 %collective-permute-start.11 = (bf16[512,128]{1,0:T(8,128)(2,1)S(1)}, bf16[512,128]{1,0:T(8,128)(2,1)S(1)}, u32[]{:S(2)}, u32[]{:S(2)}) collective-permute-start(bf16[512,128]{1,0:T(8,128)(2,1)S(1)} %first.1.refs_0_), channel_id=1, source_target_pairs={{0,2},{1,3},{2,0},{3,1},{4,6},{5,7},{6,4},{7,5},{8,10},{9,11},{10,... | collective-permute-start | bytes 393224 | tf_op jit(solution)/shard_map/ppermute | solution.py:168
  24.9 9.0 %collective-permute-start.10 = (bf16[512,128]{1,0:T(8,128)(2,1)S(1)}, bf16[512,128]{1,0:T(8,128)(2,1)S(1)}, u32[]{:S(2)}, u32[]{:S(2)}) collective-permute-start(bf16[512,128]{1,0:T(8,128)(2,1)S(1)} %first.1.refs_0_), channel_id=1, source_target_pairs={{0,1},{1,0},{2,3},{3,2},{4,5},{5,4},{6,7},{7,6},{8,9},{9,8},{10,11... | collective-permute-start | bytes 393224 | tf_op jit(solution)/shard_map/ppermute | solution.py:168
  27.4 6.6 %collective-permute-start.16 = (bf16[512,128]{1,0:T(8,128)(2,1)S(1)}, bf16[512,128]{1,0:T(8,128)(2,1)S(1)}, u32[]{:S(2)}, u32[]{:S(2)}) collective-permute-start(bf16[512,128]{1,0:T(8,128)(2,1)S(1)} %collective-permute-done.15.refs_6_), channel_id=1, source_target_pairs={{0,1},{1,0},{2,3},{3,2},{4,5},{5,4},{6,7},{7,6},{8,9},{9,8},{10,11... | collective-permute-start | bytes 393224 | tf_op jit(solution)/shard_map/ppermute | solution.py:168
  27.4 14.3 %collective-permute-start.17 = (bf16[256,512]{1,0:T(8,128)(2,1)S(1)}, bf16[256,512]{1,0:T(8,128)(2,1)S(1)}, u32[]{:S(2)}, u32[]{:S(2)}) collective-permute-start(bf16[256,512]{1,0:T(8,128)(2,1)S(1)} %get-tuple-element.15), channel_id=1, source_target_pairs={{0,8},{8,0},{16,24},{24,16},{1,9},{9,1},{17,25},{25,17},{2,10},{10... | collective-permute-start | bytes 786440 | tf_op jit(solution)/shard_map/ppermute | solution.py:168
  30.2 21.6 %collective-permute-start.18 = (bf16[256,512]{1,0:T(8,128)(2,1)S(1)}, bf16[256,512]{1,0:T(8,128)(2,1)S(1)}, u32[]{:S(2)}, u32[]{:S(2)}) collective-permute-start(bf16[256,512]{1,0:T(8,128)(2,1)S(1)} %get-tuple-element.16), channel_id=1, source_target_pairs={{0,16},{8,24},{16,0},{24,8},{1,17},{9,25},{17,1},{25,9},{2,18},{10... | collective-permute-start | bytes 786440 | tf_op jit(solution)/shard_map/ppermute | solution.py:168
  33.9 22.8 %collective-permute-start.19 = (bf16[256,512]{1,0:T(8,128)(2,1)S(1)}, bf16[256,512]{1,0:T(8,128)(2,1)S(1)}, u32[]{:S(2)}, u32[]{:S(2)}) collective-permute-start(bf16[256,512]{1,0:T(8,128)(2,1)S(1)} %get-tuple-element.17), channel_id=1, source_target_pairs={{0,24},{8,16},{16,8},{24,0},{1,25},{9,17},{17,9},{25,1},{2,26},{10... | collective-permute-start | bytes 786440 | tf_op jit(solution)/shard_map/ppermute | solution.py:168
  33.9 1.4 %collective-permute-start.14 = (bf16[512,128]{1,0:T(8,128)(2,1)S(1)}, bf16[512,128]{1,0:T(8,128)(2,1)S(1)}, u32[]{:S(2)}, u32[]{:S(2)}) collective-permute-start(bf16[512,128]{1,0:T(8,128)(2,1)S(1)} %collective-permute-done.13.refs_4_), channel_id=1, source_target_pairs={{0,1},{1,0},{2,3},{3,2},{4,5},{5,4},{6,7},{7,6},{8,9},{9,8},{10,11... | collective-permute-start | bytes 393224 | tf_op jit(solution)/shard_map/ppermute | solution.py:168
  34.0 1.5 %collective-permute-start.12 = (bf16[512,128]{1,0:T(8,128)(2,1)S(1)}, bf16[512,128]{1,0:T(8,128)(2,1)S(1)}, u32[]{:S(2)}, u32[]{:S(2)}) collective-permute-start(bf16[512,128]{1,0:T(8,128)(2,1)S(1)} %collective-permute-done.11.refs_2_), channel_id=1, source_target_pairs={{0,1},{1,0},{2,3},{3,2},{4,5},{5,4},{6,7},{7,6},{8,9},{9,8},{10,11... | collective-permute-start | bytes 393224 | tf_op jit(solution)/shard_map/ppermute | solution.py:168
